TPU v7x, 512 devices: a whole 4x4x16 slice. The times are simulated.
512 devices in a mesh: section: 8 (over x_lo, y), seq: 64 (over x_hi, z, core).
Axes of the slice: x: 4 (x_hi: 2, x_lo: 2; x = x_hi * 2 + x_lo), y: 4, z: 16, core: 2. Of those that a mesh axis runs over, the one named last changes fastest.
Arguments:
- resident_microbatches: bfloat16 [8, 8192, 1024], P('section', 'seq'), may hold values from -64 to 64
- arriving_microbatch: bfloat16 [8192, 1024], P('seq'), may hold values from -64 to 64
- prenormal_scaling: float32 [8, 1024], P('section'), may hold values from 0.1 to 1.9
- attention_triple_matrix: bfloat16 [8, 1024, 3072], P('section', 'seq'), may hold values from -0.1875 to 0.1875
- exit_projection_matrix: bfloat16 [8, 1024, 1024], P('section'), may hold values from -0.1875 to 0.1875
- mirrored_lookup_tile: int32 [64, 4], replicated, may hold values from 0 to 1
Outputs:
- tick_out: bfloat16 [2, 8, 8192, 1024], P(None, 'section', 'seq')
All inputs are finite; a program needn't handle non-finite values.
Results may differ from a plain program's by a relative error of at most 0.004.
Values may be sent and summed in bfloat16 or wider, within the bound.
A program may use at most 64 MiB of HBM per device.

v0:
```python
import jax
import jax.numpy as jnp
from jax import lax
from jax.sharding import PartitionSpec as P

HEADS = 8
HEAD = 128
BLOCK = 64
LEVELS = 4


epsilon = 1e-06


def swapped(x, axis, stride):
    return lax.ppermute(x, axis, [(i, i ^ 1 << stride) for i in range(lax.axis_size(axis))])


def from_behind(block, axis, distance):
    devices = range(lax.axis_size(axis))
    route = [(i - distance, i) for i in devices if i - distance in devices]
    return lax.ppermute(block, axis, route)


def head_norm(projected, row_count):
    shaped = projected.reshape(row_count, HEADS, HEAD)
    mean_square = jnp.mean(shaped * shaped, axis=-1, keepdims=True)
    return (shaped * lax.rsqrt(mean_square + epsilon)).astype(jnp.bfloat16)


def transform_through_tier(
    hidden_in, gain_row, weights, out_weights, mirrored_lookup_tile, compute_unit
):
    row_count = hidden_in.shape[0]
    blocks = row_count // BLOCK
    inner_width = HEADS * HEAD
    widened = hidden_in.astype(jnp.float32)
    mean_square = jnp.mean(widened * widened, axis=-1, keepdims=True)
    normed = (widened * lax.rsqrt(mean_square + epsilon) * gain_row).astype(jnp.bfloat16)
    projected = jnp.dot(normed, weights, preferred_element_type=jnp.float32)
    queries = head_norm(projected[:, :inner_width], row_count)
    key_rows = head_norm(projected[:, inner_width : 2 * inner_width], row_count).reshape(
        row_count, inner_width
    )
    values = projected[:, 2 * inner_width :].astype(jnp.bfloat16)
    key_value = jnp.stack([key_rows, values])
    remote = []
    for bit_level in range(LEVELS):
        arrived = swapped(key_value, "seq", bit_level)
        wanted = mirrored_lookup_tile[compute_unit, bit_level]
        remote.append(lax.dynamic_slice_in_dim(arrived, wanted * BLOCK, BLOCK, 1))
    remote = jnp.concatenate(remote, axis=1)
    far_keys = jnp.broadcast_to(
        remote[0].reshape(1, LEVELS * BLOCK, HEADS, HEAD), (blocks, LEVELS * BLOCK, HEADS, HEAD)
    )
    far_values = jnp.broadcast_to(
        remote[1].reshape(1, LEVELS * BLOCK, HEADS, HEAD), (blocks, LEVELS * BLOCK, HEADS, HEAD)
    )
    query_blocks = queries.reshape(blocks, BLOCK, HEADS, HEAD)
    all_keys = jnp.concatenate([key_rows.reshape(blocks, BLOCK, HEADS, HEAD), far_keys], axis=1)
    all_values = jnp.concatenate([values.reshape(blocks, BLOCK, HEADS, HEAD), far_values], axis=1)
    score_scale = HEAD ** (-0.5)
    scores = (
        jnp.einsum("cqhd,ckhd->chqk", query_blocks, all_keys, preferred_element_type=jnp.float32)
        * score_scale
    )
    exps = jnp.exp(scores)
    weights_soft = (exps / jnp.sum(exps, axis=-1, keepdims=True)).astype(jnp.bfloat16)
    mixed_heads = jnp.einsum(
        "chqk,ckhd->cqhd", weights_soft, all_values, preferred_element_type=jnp.float32
    )
    attended = mixed_heads.astype(jnp.bfloat16).reshape(row_count, inner_width)
    return (widened + jnp.dot(attended, out_weights, preferred_element_type=jnp.float32)).astype(
        jnp.bfloat16
    )


def per_device(
    resident_microbatches,
    arriving_microbatch,
    prenormal_scaling,
    attention_triple_matrix,
    exit_projection_matrix,
    mirrored_lookup_tile,
):
    layer_parameters = lax.all_gather(attention_triple_matrix[0], "seq", axis=0, tiled=True)
    compute_unit = lax.axis_index("seq")
    section_index = lax.axis_index("section")
    starting_result = transform_through_tier(
        resident_microbatches[0],
        prenormal_scaling[0],
        layer_parameters,
        exit_projection_matrix[0],
        mirrored_lookup_tile,
        compute_unit,
    )
    moved = from_behind(starting_result, "section", 1)
    second_in = jnp.where(section_index == 0, arriving_microbatch, moved)
    second_out = transform_through_tier(
        second_in,
        prenormal_scaling[0],
        layer_parameters,
        exit_projection_matrix[0],
        mirrored_lookup_tile,
        compute_unit,
    )
    return jnp.stack([starting_result, second_out])[:, None]


def solution(mesh):
    placed = (
        P("section", "seq", None),
        P("seq", None),
        P("section", None),
        P("section", "seq", None),
        P("section", None, None),
        P(),
    )
    return jax.shard_map(
        per_device,
        mesh=mesh,
        in_specs=placed,
        out_specs=P(None, "section", "seq", None),
        check_vma=False,
    )
```

profile of v0, /device:TPU:34, one launch (start us, length us, event | category | flops | bytes accessed | tf_op | source)
XLA Modules:
  0.0 360.5 jit_solution(13483647688169495418)
XLA Ops:
  6.5 0.7 all-gather.3.cloned.1.call-update
  7.3 1.1 fusion.54
  8.4 163.1 %all-gather.3.cloned.1.call-done = bf16[1,1024,3072]{2,1,0:T(8,128)(2,1)} async-done(((bf16[1,16,3072]{2,1,0:T(8,128)(2,1)}), bf16[1,1024,3072]{2,1,0:T(8,128)(2,1)}) %all-gather.3.cloned.1.call-update) | async-done | bytes 6291472 | tf_op jit(solution)/shard_map/all_gather | solution.py:86
  171.4 3.9 %fusion.2 = f32[128,3072]{1,0:T(8,128)S(1)} fusion(bf16[1,1024,3072]{2,1,0:T(8,128)(2,1)} %all-gather.3.cloned.1.call-done, bf16[1,128,1024]{2,1,0:T(8,128)(2,1)} %param.6, f32[1024]{0:T(1024)} %bitcast.157, f32[128]{0:T(128)S(1)} %add_rsqrt_fusion.5), kind=kOutput, calls=%fused_computation.2 | convolution fusion | flops 805830656 | bytes 8131072 | tf_op jit(solution)/shard_map/dot_general | solution.py:40
  175.4 1.1 copy-done.2
  176.7 0.2 reduce_sum.73
  177.1 0.2 mul.156
  177.3 2.4 multiply_bitcast_fusion.2
  179.7 0.9 pad_maximum_fusion.2
  180.6 3.5 collective-permute-start.2
  184.1 0.7 constant_dynamic-slice_fusion.8
  187.3 2.3 collective-permute-start.1
  189.6 1.9 collective-permute-start
  191.5 5.1 %collective-permute-start.3 = (bf16[2,128,1024]{2,1,0:T(8,128)(2,1)}, bf16[2,128,1024]{2,1,0:T(8,128)(2,1)}, u32[]{:S(2)}, u32[]{:S(2)}) collective-permute-start(bf16[2,128,1024]{2,1,0:T(8,128)(2,1)} %pad_maximum_fusion.2), channel_id=1, source_target_pairs={{0,8},{1,9},{2,10},{3,11},{4,12},{5,13},{6,14},{7,15},{8,0},{9,1},... | collective-permute-start | bytes 1572872 | tf_op jit(solution)/shard_map/ppermute | solution.py:16
  196.6 1.1 copy.82
  197.7 0.2 reduce_sum.74
  198.1 1.2 copy.83
  199.5 0.8 copy.61
  200.2 0.2 fusion.61
  200.5 7.2 %collective-permute-done.2 = bf16[2,128,1024]{2,1,0:T(8,128)(2,1)} collective-permute-done((bf16[2,128,1024]{2,1,0:T(8,128)(2,1)}, bf16[2,128,1024]{2,1,0:T(8,128)(2,1)}, u32[]{:S(2)}, u32[]{:S(2)}) %collective-permute-start.2) | collective-permute-done | bytes 524320 | tf_op jit(solution)/shard_map/ppermute | solution.py:16
  207.7 1.0 constant_dynamic-slice_fusion.5
  208.6 12.4 %collective-permute-done.1 = bf16[2,128,1024]{2,1,0:T(8,128)(2,1)} collective-permute-done((bf16[2,128,1024]{2,1,0:T(8,128)(2,1)}, bf16[2,128,1024]{2,1,0:T(8,128)(2,1)}, u32[]{:S(2)}, u32[]{:S(2)}) %collective-permute-start.1) | collective-permute-done | bytes 524320 | tf_op jit(solution)/shard_map/ppermute | solution.py:16
  221.0 1.0 constant_dynamic-slice_fusion.6
  222.0 1.0 constant_dynamic-slice_fusion.7
  223.0 25.9 %collective-permute-done.3 = bf16[2,128,1024]{2,1,0:T(8,128)(2,1)} collective-permute-done((bf16[2,128,1024]{2,1,0:T(8,128)(2,1)}, bf16[2,128,1024]{2,1,0:T(8,128)(2,1)}, u32[]{:S(2)}, u32[]{:S(2)}) %collective-permute-start.3) | collective-permute-done | bytes 524320 | tf_op jit(solution)/shard_map/ppermute | solution.py:16
  248.9 1.0 constant_dynamic-slice_fusion.4
  250.4 0.2 broadcast_in_dim.42
  250.6 1.8 multiply_exponential_fusion.1
  252.4 0.2 broadcast_in_dim.19
  252.6 3.2 fusion.43
  255.8 1.1 copy.68
  256.9 0.4 fusion.37
  257.4 3.5 collective-permute-start.4
  260.9 7.8 %collective-permute-done.4 = bf16[128,1024]{1,0:T(8,128)(2,1)S(1)} collective-permute-done((bf16[128,1024]{1,0:T(8,128)(2,1)S(1)}, bf16[128,1024]{1,0:T(8,128)(2,1)S(1)}, u32[]{:S(2)}, u32[]{:S(2)}) %collective-permute-start.4) | collective-permute-done | bytes 262176 | tf_op jit(solution)/shard_map/ppermute | solution.py:22
  268.9 3.8 %fusion = f32[128,3072]{1,0:T(8,128)S(1)} fusion(bf16[1,1024,3072]{2,1,0:T(8,128)(2,1)} %all-gather.3.cloned.1.call-done, bf16[128,1024]{1,0:T(8,128)(2,1)S(1)} %get-tuple-element.6, f32[128]{0:T(128)S(1)} %add_rsqrt_fusion.4, f32[1024]{0:T(1024)S(1)} %bitcast.158), kind=kOutput, calls=%fused_computation | convolution fusion | flops 805830656 | bytes 8131072 | tf_op jit(solution)/shard_map/dot_general | solution.py:40
  272.8 1.1 copy-done.1
  273.9 0.9 fusion.82
  274.9 0.2 reduce_sum.77
  275.3 0.2 mul.180
  275.5 2.2 multiply_bitcast_fusion
  277.8 0.8 pad_maximum_fusion.3
  278.6 1.9 collective-permute-start.7
  280.5 2.0 collective-permute-start.6
  282.5 1.9 collective-permute-start.5
  284.6 0.2 reduce_sum.78
  284.9 8.3 %collective-permute-start.8 = (bf16[2,128,1024]{2,1,0:T(8,128)(2,1)}, bf16[2,128,1024]{2,1,0:T(8,128)(2,1)}, u32[]{:S(2)}, u32[]{:S(2)}) collective-permute-start(bf16[2,128,1024]{2,1,0:T(8,128)(2,1)} %pad_maximum_fusion.3), channel_id=1, source_target_pairs={{0,8},{1,9},{2,10},{3,11},{4,12},{5,13},{6,14},{7,15},{8,0},{9,1},... | collective-permute-start | bytes 1572872 | tf_op jit(solution)/shard_map/ppermute | solution.py:16
  293.2 1.1 copy.92
  294.6 1.0 copy.96
  295.6 0.8 copy.72
  296.3 0.2 fusion.59
  296.5 8.6 %collective-permute-done.7 = bf16[2,128,1024]{2,1,0:T(8,128)(2,1)} collective-permute-done((bf16[2,128,1024]{2,1,0:T(8,128)(2,1)}, bf16[2,128,1024]{2,1,0:T(8,128)(2,1)}, u32[]{:S(2)}, u32[]{:S(2)}) %collective-permute-start.7) | collective-permute-done | bytes 524320 | tf_op jit(solution)/shard_map/ppermute | solution.py:16
  305.1 1.0 constant_dynamic-slice_fusion.1
  306.1 1.0 constant_dynamic-slice_fusion.2
  307.1 1.0 constant_dynamic-slice_fusion.3
  308.0 35.8 %collective-permute-done.8 = bf16[2,128,1024]{2,1,0:T(8,128)(2,1)} collective-permute-done((bf16[2,128,1024]{2,1,0:T(8,128)(2,1)}, bf16[2,128,1024]{2,1,0:T(8,128)(2,1)}, u32[]{:S(2)}, u32[]{:S(2)}) %collective-permute-start.8) | collective-permute-done | bytes 524320 | tf_op jit(solution)/shard_map/ppermute | solution.py:16
  343.9 1.0 constant_dynamic-slice_fusion
  345.4 0.2 broadcast_in_dim.46
  345.6 1.8 multiply_exponential_fusion
  347.4 0.2 broadcast_in_dim.44
  347.6 3.2 fusion.46
  350.7 1.1 copy.79
  351.9 0.4 fusion.40
  352.3 0.5 copy-done.6
  352.8 0.8 maximum_bitcast_fusion
  (63 shorter events, 2.7 us)
Async XLA Ops:
  6.5 250.4 %copy-start = (bf16[1,1024,1024]{2,1,0:T(8,128)(2,1)S(1)}, bf16[1,1024,1024]{2,1,0:T(8,128)(2,1)}, u32[]{:S(2)}) copy-start(bf16[1,1024,1024]{2,1,0:T(8,128)(2,1)} %param.10) | copy-start | bytes 6291460
  6.5 164.9 %all-gather.3.cloned.1.call-start = ((), (), s32[]{:S(2)}) async-start(), calls=%async_computation | async-start | bytes 6389760 | tf_op jit(solution)/shard_map/all_gather | solution.py:86
  175.4 1.1 copy-start.2
  177.3 6.8 %copy-start.9 = (s32[64,4]{0,1:T(4,128)S(1)}, s32[64,4]{0,1:T(4,128)}, u32[]{:S(2)}) copy-start(s32[64,4]{0,1:T(4,128)} %param.11) | copy-start | bytes 3076
  180.6 27.1 %collective-permute-start.2 = (bf16[2,128,1024]{2,1,0:T(8,128)(2,1)}, bf16[2,128,1024]{2,1,0:T(8,128)(2,1)}, u32[]{:S(2)}, u32[]{:S(2)}) collective-permute-start(bf16[2,128,1024]{2,1,0:T(8,128)(2,1)} %pad_maximum_fusion.2), channel_id=1, source_target_pairs={{0,4},{1,5},{2,6},{3,7},{4,0},{5,1},{6,2},{7,3},{8,12},{9,13},{10,... | collective-permute-start | bytes 1572872 | tf_op jit(solution)/shard_map/ppermute | solution.py:16
  187.3 33.8 %collective-permute-start.1 = (bf16[2,128,1024]{2,1,0:T(8,128)(2,1)}, bf16[2,128,1024]{2,1,0:T(8,128)(2,1)}, u32[]{:S(2)}, u32[]{:S(2)}) collective-permute-start(bf16[2,128,1024]{2,1,0:T(8,128)(2,1)} %pad_maximum_fusion.2), channel_id=1, source_target_pairs={{0,2},{1,3},{2,0},{3,1},{4,6},{5,7},{6,4},{7,5},{8,10},{9,11},{10,... | collective-permute-start | bytes 1572872 | tf_op jit(solution)/shard_map/ppermute | solution.py:16
  189.6 32.4 %collective-permute-start = (bf16[2,128,1024]{2,1,0:T(8,128)(2,1)}, bf16[2,128,1024]{2,1,0:T(8,128)(2,1)}, u32[]{:S(2)}, u32[]{:S(2)}) collective-permute-start(bf16[2,128,1024]{2,1,0:T(8,128)(2,1)} %pad_maximum_fusion.2), channel_id=1, source_target_pairs={{0,1},{1,0},{2,3},{3,2},{4,5},{5,4},{6,7},{7,6},{8,9},{9,8},{10,11... | collective-permute-start | bytes 1572872 | tf_op jit(solution)/shard_map/ppermute | solution.py:16
  191.5 57.4 %collective-permute-start.3 = (bf16[2,128,1024]{2,1,0:T(8,128)(2,1)}, bf16[2,128,1024]{2,1,0:T(8,128)(2,1)}, u32[]{:S(2)}, u32[]{:S(2)}) collective-permute-start(bf16[2,128,1024]{2,1,0:T(8,128)(2,1)} %pad_maximum_fusion.2), channel_id=1, source_target_pairs={{0,8},{1,9},{2,10},{3,11},{4,12},{5,13},{6,14},{7,15},{8,0},{9,1},... | collective-permute-start | bytes 1572872 | tf_op jit(solution)/shard_map/ppermute | solution.py:16
  252.6 4.4 %copy-start.3 = (bf16[1,128,1024]{2,1,0:T(8,128)(2,1)S(1)}, bf16[1,128,1024]{2,1,0:T(8,128)(2,1)}, u32[]{:S(2)}) copy-start(bf16[1,128,1024]{2,1,0:T(8,128)(2,1)} %param.6) | copy-start | bytes 786436
  256.9 11.8 %copy-start.7 = (bf16[128,1024]{1,0:T(8,128)(2,1)S(1)}, bf16[128,1024]{1,0:T(8,128)(2,1)}, u32[]{:S(2)}) copy-start(bf16[128,1024]{1,0:T(8,128)(2,1)} %param.7) | copy-start | bytes 786436
  256.9 12.0 %copy-start.8 = (f32[1,1024]{1,0:T(1,128)S(1)}, f32[1,1024]{1,0:T(1,128)}, u32[]{:S(2)}) copy-start(f32[1,1024]{1,0:T(1,128)} %param.8) | copy-start | bytes 12292
  257.4 15.4 %copy-start.5 = (bf16[128,1024]{1,0:T(8,128)(2,1)}, bf16[128,1024]{1,0:T(8,128)(2,1)S(1)}, u32[]{:S(2)}) copy-start(bf16[128,1024]{1,0:T(8,128)(2,1)S(1)} %fusion.37) | copy-start | bytes 786436
  257.4 11.3 %collective-permute-start.4 = (bf16[128,1024]{1,0:T(8,128)(2,1)S(1)}, bf16[128,1024]{1,0:T(8,128)(2,1)S(1)}, u32[]{:S(2)}, u32[]{:S(2)}) collective-permute-start(bf16[128,1024]{1,0:T(8,128)(2,1)S(1)} %fusion.37), channel_id=1, source_target_pairs={{0,64},{64,128},{128,192},{192,256},{256,320},{320,384},{384,448},... | collective-permute-start | bytes 786440 | tf_op jit(solution)/shard_map/ppermute | solution.py:22
  272.8 1.2 copy-start.1
  275.5 2.3 copy-start.4
  278.6 26.5 %collective-permute-start.7 = (bf16[2,128,1024]{2,1,0:T(8,128)(2,1)}, bf16[2,128,1024]{2,1,0:T(8,128)(2,1)}, u32[]{:S(2)}, u32[]{:S(2)}) collective-permute-start(bf16[2,128,1024]{2,1,0:T(8,128)(2,1)} %pad_maximum_fusion.3), channel_id=1, source_target_pairs={{0,4},{1,5},{2,6},{3,7},{4,0},{5,1},{6,2},{7,3},{8,12},{9,13},{10,... | collective-permute-start | bytes 1572872 | tf_op jit(solution)/shard_map/ppermute | solution.py:16
  280.5 25.5 %collective-permute-start.6 = (bf16[2,128,1024]{2,1,0:T(8,128)(2,1)}, bf16[2,128,1024]{2,1,0:T(8,128)(2,1)}, u32[]{:S(2)}, u32[]{:S(2)}) collective-permute-start(bf16[2,128,1024]{2,1,0:T(8,128)(2,1)} %pad_maximum_fusion.3), channel_id=1, source_target_pairs={{0,2},{1,3},{2,0},{3,1},{4,6},{5,7},{6,4},{7,5},{8,10},{9,11},{10,... | collective-permute-start | bytes 1572872 | tf_op jit(solution)/shard_map/ppermute | solution.py:16
  282.5 24.5 %collective-permute-start.5 = (bf16[2,128,1024]{2,1,0:T(8,128)(2,1)}, bf16[2,128,1024]{2,1,0:T(8,128)(2,1)}, u32[]{:S(2)}, u32[]{:S(2)}) collective-permute-start(bf16[2,128,1024]{2,1,0:T(8,128)(2,1)} %pad_maximum_fusion.3), channel_id=1, source_target_pairs={{0,1},{1,0},{2,3},{3,2},{4,5},{5,4},{6,7},{7,6},{8,9},{9,8},{10,11... | collective-permute-start | bytes 1572872 | tf_op jit(solution)/shard_map/ppermute | solution.py:16
  284.9 59.0 %collective-permute-start.8 = (bf16[2,128,1024]{2,1,0:T(8,128)(2,1)}, bf16[2,128,1024]{2,1,0:T(8,128)(2,1)}, u32[]{:S(2)}, u32[]{:S(2)}) collective-permute-start(bf16[2,128,1024]{2,1,0:T(8,128)(2,1)} %pad_maximum_fusion.3), channel_id=1, source_target_pairs={{0,8},{1,9},{2,10},{3,11},{4,12},{5,13},{6,14},{7,15},{8,0},{9,1},... | collective-permute-start | bytes 1572872 | tf_op jit(solution)/shard_map/ppermute | solution.py:16
  351.9 1.0 copy-start.6
Sparse Core Ops, SparseCore 0:
  10.6 160.7 all-gather.2
where the time goes:
time: 362 us; the launch traced here: 360 us
  waiting for transfers between devices  261 us (72%)
  starting transfers between devices  30.4 us (8%)
  local copies, waits for them, and re-layouts  23.6 us (7%)
  matrix products  18.6 us (5%)
  between operations  16.4 us (5%)
  other arithmetic  9.93 us (3%)
    all_gather x1, waiting for transfers between devices, per_device(): lax.all_gather(attention_triple_matrix[0], 'seq', axis=0, tiled=True)  163 us
    ppermute x8, waiting for transfers between devices, swapped(): lax.ppermute(x, axis, [(i, i ^ 1 << stride) for i in range(lax.axis_size(...  89.9 us
    ppermute x8, starting transfers between devices, swapped(): lax.ppermute(x, axis, [(i, i ^ 1 << stride) for i in range(lax.axis_size(...  27 us
    unnamed x38, local copies, waits for them, and re-layouts  9.15 us
    ppermute x1, waiting for transfers between devices, from_behind(): return lax.ppermute(block, axis, route)  7.83 us
    dynamic_slice x8, local copies, waits for them, and re-layouts, transform_through_tier(): remote.append(lax.dynamic_slice_in_dim(arrived, wanted * BLOCK, BLOCK, 1))  7.78 us
    dot_general x2, matrix products, transform_through_tier(): projected = jnp.dot(normed, weights, preferred_element_type=jnp.float32)  7.77 us
  transfers between devices with their start and end apart: 10, of which 7 were waited for; matrix products, arithmetic and copies ran while one was open for 4% of the time, Pallas kernels for 0%

commit v1 on v0

v1 whole, which is shorter than its diff:
```python
import jax
import jax.numpy as jnp
from jax import lax
from jax.experimental import pallas as pl
from jax.experimental.pallas import tpu as pltpu
from jax.sharding import PartitionSpec as P

HEADS = 8
HEAD = 128
BLOCK = 64
LEVELS = 4
NZ = 16
RUN = 128
D = 1024
INNER = 1024
SHARD = 16
PASSES = 4
PCOLS = 768
PW = 256
ROWS = RUN + LEVELS * BLOCK
EPS = 1e-06

BOTH = (False, False, False, False)


def flip(i, bit):
    step = 1 << bit
    return i + step * (1 - 2 * ((i // step) % 2))


def kernel(
    sections,
    x_hbm,
    arr_hbm,
    gain_ref,
    w_hbm,
    wo_hbm,
    table_ref,
    out_hbm,
    wbuf,
    wo,
    x1,
    x2,
    arr,
    nrm,
    att,
    send1,
    send2,
    o1,
    o2,
    rbuf,
    load_sem,
    z_recv,
    x_recv,
    sib_recv,
    z_send,
    x_send,
    sib_send,
    e_send,
    e_recv,
    r_send,
    r_recv,
    out_sem,
):
    sec = lax.axis_index("section")
    me = lax.axis_index("seq")
    h = me // (2 * NZ)
    z = (me // 2) % NZ
    c = me % 2
    nxt = (sec + 1) % sections
    prv = (sec + sections - 1) % sections

    def at(hh, zz, cc):
        return hh * (2 * NZ) + zz * 2 + cc

    up = at(h, (z + 1) % NZ, c)
    down = at(h, (z + NZ - 1) % NZ, c)
    sib = flip(me, 0)
    across = at(1 - h, z, c)
    partners = [flip(me, b) for b in range(LEVELS)]

    def dev(s, j):
        return {"section": s, "seq": j}

    barrier = pltpu.get_barrier_semaphore()
    talk = [(sec, up), (sec, down), (sec, sib), (sec, across)]
    talk += [(sec, partners[b]) for b in range(1, LEVELS)]
    talk += [(prv, me)] + [(prv, partners[b]) for b in range(1, LEVELS)]
    for s, j in talk:
        pl.semaphore_signal(barrier, inc=1, device_id=dev(s, j))

    def choose(ref, reader, level):
        second = jnp.full((BLOCK, D), table_ref[reader, level], jnp.int32) > 0
        lower = ref[pl.ds(0, BLOCK), :].astype(jnp.float32)
        upper = ref[pl.ds(BLOCK, BLOCK), :].astype(jnp.float32)
        return jnp.where(second, upper, lower).astype(jnp.bfloat16)

    def rows(slot):
        return pl.ds(pl.multiple_of(slot * SHARD, SHARD), SHARD)

    loads = []
    for p in range(PASSES):
        for g in range(3):
            loads.append(
                pltpu.make_async_copy(
                    w_hbm.at[0, :, pl.ds(g * INNER + p * PW, PW)],
                    wbuf.at[rows(me), pl.ds(p * PCOLS + g * PW, PW)],
                    load_sem.at[p * 3 + g],
                )
            )
    load_x = pltpu.make_async_copy(x_hbm.at[0], x1.at[pl.ds(0, RUN)], load_sem.at[12])
    load_arr = pltpu.make_async_copy(arr_hbm, arr, load_sem.at[13])
    load_wo = pltpu.make_async_copy(wo_hbm.at[0], wo, load_sem.at[14])
    load_x.start()
    for cp in loads:
        cp.start()
    load_arr.start()
    load_wo.start()
    load_x.wait()
    for b in range(LEVELS):
        send1[b] = choose(x1, partners[b], b)
    for cp in loads:
        cp.wait()
    pl.semaphore_wait(barrier, len(talk))

    def cols(p):
        return pl.ds(p * PCOLS, PCOLS)

    def piece(slot, p):
        return wbuf.at[rows(slot), cols(p)]

    def push(slot, p, send, recv, target):
        pltpu.make_async_remote_copy(
            src_ref=piece(slot, p),
            dst_ref=piece(slot, p),
            send_sem=send,
            recv_sem=recv,
            device_id=dev(sec, target),
        ).start()

    def got(slot, p, recv):
        pltpu.make_async_copy(piece(slot, p), piece(slot, p), recv).wait()

    def to_sib(slot, p):
        push(slot, p, sib_send.at[p], sib_recv.at[p], sib)

    def zsem(col, d, s, p):
        return z_recv.at[((col * 2 + d) * 9 + s) * PASSES + p]

    def xsem(s, d, p):
        return x_recv.at[(d * 9 + s) * PASSES + p]

    def exch(b, src, dst, send, recv, s, j):
        return pltpu.make_async_remote_copy(
            src_ref=src, dst_ref=dst, send_sem=send, recv_sem=recv, device_id=dev(s, j)
        )

    e1 = [
        exch(
            b,
            send1.at[b],
            x1.at[pl.ds(RUN + b * BLOCK, BLOCK)],
            e_send.at[b],
            e_recv.at[b],
            sec,
            partners[b],
        )
        for b in range(LEVELS)
    ]

    for p in range(PASSES):
        push(me, p, z_send.at[p], zsem(0, 0, 1, p), up)
        push(me, p, z_send.at[p], zsem(0, 1, 1, p), down)
        to_sib(me, p)
        push(me, p, x_send.at[p], xsem(0, 0, p), across)
    for b in range(LEVELS):
        e1[b].start()

    for p in range(PASSES):
        if BOTH[p]:
            got(across, p, xsem(0, 0, p))
            push(across, p, z_send.at[p], zsem(1, 0, 1, p), up)
            push(across, p, z_send.at[p], zsem(1, 1, 1, p), down)
            to_sib(across, p)

    def arrivals(s, full, last):
        below = at(h, (z + NZ - s) % NZ, c)
        above = at(h, (z + s) % NZ, c)
        for p in range(PASSES):
            for col in range(2 if BOTH[p] else 1):
                shift = (1 - 2 * h) * (2 * NZ) * col
                got(below + shift, p, zsem(col, 0, s, p))
                if not last:
                    push(below + shift, p, z_send.at[p], zsem(col, 0, s + 1, p), up)
                if not BOTH[p]:
                    push(below, p, x_send.at[p], xsem(s, 0, p), across)
                to_sib(below + shift, p)
                if not last:
                    got(above + shift, p, zsem(col, 1, s, p))
                    if full:
                        push(above + shift, p, z_send.at[p], zsem(col, 1, s + 1, p), down)
                    if not BOTH[p]:
                        push(above, p, x_send.at[p], xsem(s, 1, p), across)
                    to_sib(above + shift, p)

    def crossed(s, two):
        below = at(1 - h, (z + NZ - s) % NZ, c)
        above = at(1 - h, (z + s) % NZ, c)
        for p in range(PASSES):
            if not BOTH[p]:
                got(below, p, xsem(s, 0, p))
                to_sib(below, p)
                if two:
                    got(above, p, xsem(s, 1, p))
                    to_sib(above, p)

    def step(s, carry):
        arrivals(s, True, False)

        @pl.when(s == 1)
        def _():
            crossed(0, False)

        @pl.when(s > 1)
        def _():
            crossed(s - 1, True)

        return carry

    lax.fori_loop(1, NZ // 2 - 1, step, 0)
    arrivals(NZ // 2 - 1, False, False)
    crossed(NZ // 2 - 2, True)
    arrivals(NZ // 2, False, True)
    crossed(NZ // 2 - 1, True)
    crossed(NZ // 2, False)

    qrow = lax.broadcasted_iota(jnp.int32, (RUN, ROWS), 0)
    kcol = lax.broadcasted_iota(jnp.int32, (RUN, ROWS), 1)
    seen = (kcol >= RUN) | ((kcol >= BLOCK) == (qrow >= BLOCK))
    mask = jnp.where(seen, 1.0, 0.0).astype(jnp.float32)

    def unit(a):
        ms = jnp.mean(a * a, axis=-1, keepdims=True)
        return (a * lax.rsqrt(ms + EPS)).astype(jnp.bfloat16)

    def normalise(xr, start, count):
        wide = xr[pl.ds(start, count), :].astype(jnp.float32)
        ms = jnp.mean(wide * wide, axis=-1, keepdims=True)
        nrm[pl.ds(start, count), :] = (wide * lax.rsqrt(ms + EPS) * gain_ref[...]).astype(
            jnp.bfloat16
        )

    def layer(xr, outv, tick):
        def group(p, carry):
            base = pl.multiple_of(p * PCOLS, PCOLS)
            q = jnp.dot(
                nrm[pl.ds(0, RUN), :], wbuf[:, pl.ds(base, PW)], preferred_element_type=jnp.float32
            )
            k = jnp.dot(
                nrm[...], wbuf[:, pl.ds(base + PW, PW)], preferred_element_type=jnp.float32
            )
            v = jnp.dot(
                nrm[...], wbuf[:, pl.ds(base + 2 * PW, PW)], preferred_element_type=jnp.float32
            ).astype(jnp.bfloat16)
            for i in range(PW // HEAD):
                lanes = slice(i * HEAD, (i + 1) * HEAD)
                score = lax.dot_general(
                    unit(q[:, lanes]),
                    unit(k[:, lanes]),
                    (((1,), (1,)), ((), ())),
                    preferred_element_type=jnp.float32,
                ) * (HEAD ** (-0.5))
                e = jnp.exp(score) * mask
                weight = (e / jnp.sum(e, axis=-1, keepdims=True)).astype(jnp.bfloat16)
                att[:, pl.ds(pl.multiple_of(p * PW + i * HEAD, HEAD), HEAD)] = jnp.dot(
                    weight, v[:, lanes], preferred_element_type=jnp.float32
                ).astype(jnp.bfloat16)
            return carry

        lax.fori_loop(0, PASSES, group, 0)

        def project(n, carry):
            lanes = pl.ds(pl.multiple_of(n * PW, PW), PW)
            outv[:, lanes] = (
                xr[pl.ds(0, RUN), lanes].astype(jnp.float32)
                + jnp.dot(att[...], wo[:, lanes], preferred_element_type=jnp.float32)
            ).astype(jnp.bfloat16)
            return carry

        lax.fori_loop(0, D // PW, project, 0)
        cp = pltpu.make_async_copy(outv, out_hbm.at[tick, 0], out_sem.at[tick])
        cp.start()
        return cp

    for b in range(LEVELS):
        e1[b].wait_recv()
    normalise(x1, 0, ROWS)
    for p in range(PASSES):
        half = wbuf.at[pl.ds(0, 512), cols(p)]
        pltpu.make_async_copy(half, half, sib_recv.at[p]).wait()
    load_wo.wait()
    load_arr.wait()
    out1 = layer(x1, o1, 0)

    rbuf[...] = jnp.where(sec == sections - 1, arr[...], o1[...])
    for b in range(1, LEVELS):
        send2[b] = choose(rbuf, partners[b], b)
    relay = exch(0, rbuf, x2.at[pl.ds(0, RUN)], r_send.at[4], r_recv.at[4], nxt, me)
    relay.start()
    e2 = [None] + [
        exch(
            b,
            send2.at[b],
            x2.at[pl.ds(RUN + b * BLOCK, BLOCK)],
            r_send.at[b],
            r_recv.at[b],
            nxt,
            partners[b],
        )
        for b in range(1, LEVELS)
    ]
    for b in (3, 2, 1):
        e2[b].start()
    relay.wait_recv()
    send2[0] = choose(x2, sib, 0)
    e2[0] = exch(
        0, send2.at[0], x2.at[pl.ds(RUN, BLOCK)], r_send.at[0], r_recv.at[0], sec, sib
    )
    e2[0].start()
    for b in range(LEVELS):
        e2[b].wait_recv()
    normalise(x2, 0, ROWS)
    out2 = layer(x2, o2, 1)

    for p in range(PASSES):
        zn = (2 * (NZ - 1)) if BOTH[p] else (NZ - 1)
        xn = 1 if BOTH[p] else NZ
        for n, sem in ((zn, z_send.at[p]), (xn, x_send.at[p]), (2 * NZ, sib_send.at[p])):
            ref = wbuf.at[pl.ds(0, n * SHARD), cols(p)]
            pltpu.make_async_copy(ref, ref, sem).wait()
    for b in range(LEVELS):
        e1[b].wait_send()
        e2[b].wait_send()
    relay.wait_send()
    out1.wait()
    out2.wait()


def per_device(sections, x, arr, gain, w, wo, table):
    import functools

    anyspec = pl.BlockSpec(memory_space=pl.ANY)
    vspec = pl.BlockSpec(memory_space=pltpu.VMEM)
    dma = pltpu.SemaphoreType.DMA
    bf = jnp.bfloat16
    return pl.pallas_call(
        functools.partial(kernel, sections),
        out_shape=jax.ShapeDtypeStruct((2, 1, RUN, D), bf),
        in_specs=[
            anyspec,
            anyspec,
            vspec,
            anyspec,
            anyspec,
            pl.BlockSpec(memory_space=pltpu.SMEM),
        ],
        out_specs=anyspec,
        scratch_shapes=[
            pltpu.VMEM((D, 3 * INNER), bf),
            pltpu.VMEM((INNER, D), bf),
            pltpu.VMEM((ROWS, D), bf),
            pltpu.VMEM((ROWS, D), bf),
            pltpu.VMEM((RUN, D), bf),
            pltpu.VMEM((ROWS, D), bf),
            pltpu.VMEM((RUN, INNER), bf),
            pltpu.VMEM((LEVELS, BLOCK, D), bf),
            pltpu.VMEM((LEVELS, BLOCK, D), bf),
            pltpu.VMEM((RUN, D), bf),
            pltpu.VMEM((RUN, D), bf),
            pltpu.VMEM((RUN, D), bf),
            dma((15,)),
            dma((4 * 9 * PASSES,)),
            dma((2 * 9 * PASSES,)),
            dma((PASSES,)),
            dma((PASSES,)),
            dma((PASSES,)),
            dma((PASSES,)),
            dma((LEVELS,)),
            dma((LEVELS,)),
            dma((LEVELS + 1,)),
            dma((LEVELS + 1,)),
            dma((2,)),
        ],
        compiler_params=pltpu.CompilerParams(
            collective_id=0, has_side_effects=True, vmem_limit_bytes=56 * 1024 * 1024
        ),
    )(x, arr, gain, w, wo, table)


def solution(mesh):
    import functools

    placed = (
        P("section", "seq", None),
        P("seq", None),
        P("section", None),
        P("section", "seq", None),
        P("section", None, None),
        P(),
    )
    return jax.shard_map(
        functools.partial(per_device, mesh.shape["section"]),
        mesh=mesh,
        in_specs=placed,
        out_specs=P(None, "section", "seq", None),
        check_vma=False,
    )
```

time: 362 us -> 99.6 us (0.28)
  the two profiles are of different devices: /device:TPU:34 before, /device:TPU:1 now
where the time goes in v1:
time: 99.6 us; the launch traced here: 99.3 us
  Pallas kernels  96 us (96%)
  local copies, waits for them, and re-layouts  3.25 us (3%)
    pallas_call x1, Pallas kernels, per_device(): pl.pallas_call(functools.partial(kernel, sections), out_shape=jax.ShapeDt...  96 us
    unnamed x2, local copies, waits for them, and re-layouts  3.25 us

profile of v1, /device:TPU:1, one launch (start us, length us, event | category | flops | bytes accessed | tf_op | source)
XLA Modules:
  0.0 99.3 jit_solution(1338990571423694860)
XLA Ops:
  0.0 1.4 %copy.7.table_ref = s32[64,4]{1,0:T(8,128)} copy(s32[64,4]{0,1:T(4,128)} %param.11) | data formatting | bytes 2048 | tf_op args[5]
  1.4 96.0 %shard_map.64 = bf16[2,1,128,1024]{3,2,1,0:T(8,128)(2,1)} custom-call(bf16[1,128,1024]{2,1,0:T(8,128)(2,1)} %x_hbm.1, bf16[128,1024]{1,0:T(8,128)(2,1)} %arr_hbm.1, f32[1,1024]{1,0:T(1,128)} %gain_ref.1, bf16[1,16,3072]{2,1,0:T(8,128)(2,1)} %w_hbm.1, bf16[1,1024,1024]{2,1,0:T(8,128)(2,1)} %wo_hbm.1, s32[64,4]{1,0:T(8,128)} %copy.7.table_ref), custom_call_target="tpu_custom_call" | custom-call | tf_op jit(solution)/shard_map/pallas_call | solution.py:356
  97.4 1.9 %copy.9 = bf16[2,1,128,1024]{3,2,1,0:T(8,128)(2,1)} copy(bf16[2,1,128,1024]{3,2,1,0:T(8,128)(2,1)} %shard_map.64) | data formatting | bytes 1048576

commit v2 on v1

--- a/solution.py
+++ b/solution.py
@@ -20,7 +20,8 @@
 ROWS = RUN + LEVELS * BLOCK
 EPS = 1e-06
 
-BOTH = (False, False, False, False)
+HOLD = ()
+EXCHANGE_AT = (5, 5, 5)
 
 
 def flip(i, bit):
@@ -32,10 +33,10 @@
     sections,
     x_hbm,
     arr_hbm,
-    gain_ref,
+    gain_hbm,
     w_hbm,
     wo_hbm,
-    table_ref,
+    table_hbm,
     out_hbm,
     wbuf,
     wo,
@@ -43,7 +44,12 @@
     x2,
     arr,
     nrm,
+    qn,
+    kn,
+    vb,
     att,
+    gain_ref,
+    table_ref,
     send1,
     send2,
     o1,
@@ -90,7 +96,10 @@
         pl.semaphore_signal(barrier, inc=1, device_id=dev(s, j))
 
     def choose(ref, reader, level):
-        second = jnp.full((BLOCK, D), table_ref[reader, level], jnp.int32) > 0
+        row = table_ref[pl.ds(level, 1), :].astype(jnp.float32)
+        here = lax.broadcasted_iota(jnp.int32, row.shape, 1) == reader
+        entry = jnp.sum(jnp.where(here, row, 0.0), axis=1, keepdims=True)
+        second = jnp.broadcast_to(entry, (BLOCK, D)) > 0.5
         lower = ref[pl.ds(0, BLOCK), :].astype(jnp.float32)
         upper = ref[pl.ds(BLOCK, BLOCK), :].astype(jnp.float32)
         return jnp.where(second, upper, lower).astype(jnp.bfloat16)
@@ -111,11 +120,16 @@
     load_x = pltpu.make_async_copy(x_hbm.at[0], x1.at[pl.ds(0, RUN)], load_sem.at[12])
     load_arr = pltpu.make_async_copy(arr_hbm, arr, load_sem.at[13])
     load_wo = pltpu.make_async_copy(wo_hbm.at[0], wo, load_sem.at[14])
+    load_gain = pltpu.make_async_copy(gain_hbm, gain_ref, load_sem.at[15])
+    load_table = pltpu.make_async_copy(table_hbm, table_ref, load_sem.at[16])
+    load_table.start()
     load_x.start()
+    load_gain.start()
     for cp in loads:
         cp.start()
     load_arr.start()
     load_wo.start()
+    load_table.wait()
     load_x.wait()
     for b in range(LEVELS):
         send1[b] = choose(x1, partners[b], b)
@@ -144,10 +158,10 @@
     def to_sib(slot, p):
         push(slot, p, sib_send.at[p], sib_recv.at[p], sib)
 
-    def zsem(col, d, s, p):
-        return z_recv.at[((col * 2 + d) * 9 + s) * PASSES + p]
-
-    def xsem(s, d, p):
+    def zsem(d, s, p):
+        return z_recv.at[(d * 9 + s) * PASSES + p]
+
+    def xsem(d, s, p):
         return x_recv.at[(d * 9 + s) * PASSES + p]
 
     def exch(b, src, dst, send, recv, s, j):
@@ -168,71 +182,93 @@
         for b in range(LEVELS)
     ]
 
-    for p in range(PASSES):
-        push(me, p, z_send.at[p], zsem(0, 0, 1, p), up)
-        push(me, p, z_send.at[p], zsem(0, 1, 1, p), down)
-        to_sib(me, p)
+    def begin():
+        for p in range(PASSES):
+            push(me, p, z_send.at[p], zsem(0, 1, p), up)
+            push(me, p, z_send.at[p], zsem(1, 1, p), down)
+        for p in range(PASSES):
+            if p not in HOLD:
+                push(me, p, x_send.at[p], xsem(0, 0, p), across)
+        for p in range(PASSES):
+            to_sib(me, p)
+
+    def held(p):
         push(me, p, x_send.at[p], xsem(0, 0, p), across)
-    for b in range(LEVELS):
-        e1[b].start()
-
-    for p in range(PASSES):
-        if BOTH[p]:
-            got(across, p, xsem(0, 0, p))
-            push(across, p, z_send.at[p], zsem(1, 0, 1, p), up)
-            push(across, p, z_send.at[p], zsem(1, 1, 1, p), down)
-            to_sib(across, p)
-
-    def arrivals(s, full, last):
+
+        def one(s, carry):
+            below = at(h, (z + NZ - s) % NZ, c)
+            above = at(h, (z + s) % NZ, c)
+            push(below, p, x_send.at[p], xsem(0, s, p), across)
+
+            @pl.when(s < NZ // 2)
+            def _():
+                push(above, p, x_send.at[p], xsem(1, s, p), across)
+
+            return carry
+
+        lax.fori_loop(1, NZ // 2 + 1, one, 0)
+
+    def ring(s):
         below = at(h, (z + NZ - s) % NZ, c)
         above = at(h, (z + s) % NZ, c)
         for p in range(PASSES):
-            for col in range(2 if BOTH[p] else 1):
-                shift = (1 - 2 * h) * (2 * NZ) * col
-                got(below + shift, p, zsem(col, 0, s, p))
-                if not last:
-                    push(below + shift, p, z_send.at[p], zsem(col, 0, s + 1, p), up)
-                if not BOTH[p]:
-                    push(below, p, x_send.at[p], xsem(s, 0, p), across)
-                to_sib(below + shift, p)
-                if not last:
-                    got(above + shift, p, zsem(col, 1, s, p))
-                    if full:
-                        push(above + shift, p, z_send.at[p], zsem(col, 1, s + 1, p), down)
-                    if not BOTH[p]:
-                        push(above, p, x_send.at[p], xsem(s, 1, p), across)
-                    to_sib(above + shift, p)
-
-    def crossed(s, two):
-        below = at(1 - h, (z + NZ - s) % NZ, c)
-        above = at(1 - h, (z + s) % NZ, c)
-        for p in range(PASSES):
-            if not BOTH[p]:
-                got(below, p, xsem(s, 0, p))
-                to_sib(below, p)
-                if two:
-                    got(above, p, xsem(s, 1, p))
-                    to_sib(above, p)
-
-    def step(s, carry):
-        arrivals(s, True, False)
-
-        @pl.when(s == 1)
-        def _():
-            crossed(0, False)
-
-        @pl.when(s > 1)
-        def _():
-            crossed(s - 1, True)
+            got(below, p, zsem(0, s, p))
+
+            @pl.when(s < NZ // 2)
+            def _():
+                push(below, p, z_send.at[p], zsem(0, s + 1, p), up)
+
+            if p not in HOLD:
+                push(below, p, x_send.at[p], xsem(0, s, p), across)
+            to_sib(below, p)
+
+            @pl.when(s < NZ // 2)
+            def _(p=p):
+                got(above, p, zsem(1, s, p))
+
+                @pl.when(s < NZ // 2 - 1)
+                def _():
+                    push(above, p, z_send.at[p], zsem(1, s + 1, p), down)
+
+                if p not in HOLD:
+                    push(above, p, x_send.at[p], xsem(1, s, p), across)
+                to_sib(above, p)
+
+    def crossed(p):
+        got(across, p, xsem(0, 0, p))
+        to_sib(across, p)
+
+        def one(s, carry):
+            below = at(1 - h, (z + NZ - s) % NZ, c)
+            above = at(1 - h, (z + s) % NZ, c)
+            got(below, p, xsem(0, s, p))
+            to_sib(below, p)
+
+            @pl.when(s < NZ // 2)
+            def _():
+                got(above, p, xsem(1, s, p))
+                to_sib(above, p)
+
+            return carry
+
+        lax.fori_loop(1, NZ // 2 + 1, one, 0)
+
+    begin()
+    e1[0].start()
+
+    def step(i, carry):
+        ring(i)
+        for b in range(1, LEVELS):
+
+            @pl.when(i == EXCHANGE_AT[b - 1])
+            def _(b=b):
+                e1[b].start()
 
         return carry
 
-    lax.fori_loop(1, NZ // 2 - 1, step, 0)
-    arrivals(NZ // 2 - 1, False, False)
-    crossed(NZ // 2 - 2, True)
-    arrivals(NZ // 2, False, True)
-    crossed(NZ // 2 - 1, True)
-    crossed(NZ // 2, False)
+    lax.fori_loop(1, NZ // 2 + 1, step, 0)
+    for p in HOLD:
+        held(p)
 
     qrow = lax.broadcasted_iota(jnp.int32, (RUN, ROWS), 0)
     kcol = lax.broadcasted_iota(jnp.int32, (RUN, ROWS), 1)
@@ -250,35 +286,42 @@
             jnp.bfloat16
         )
 
-    def layer(xr, outv, tick):
-        def group(p, carry):
-            base = pl.multiple_of(p * PCOLS, PCOLS)
+    scale = HEAD ** (-0.5)
+
+    def lanes_of(p, i):
+        return pl.ds(pl.multiple_of(p * PW + i * HEAD, HEAD), HEAD)
+
+    def prepare(p, start, count, queries):
+        base = pl.multiple_of(p * PCOLS, PCOLS)
+        if queries:
             q = jnp.dot(
                 nrm[pl.ds(0, RUN), :], wbuf[:, pl.ds(base, PW)], preferred_element_type=jnp.float32
             )
-            k = jnp.dot(
-                nrm[...], wbuf[:, pl.ds(base + PW, PW)], preferred_element_type=jnp.float32
+            for i in range(PW // HEAD):
+                qn[:, lanes_of(p, i)] = unit(q[:, i * HEAD : (i + 1) * HEAD])
+        part = nrm[pl.ds(start, count), :]
+        k = jnp.dot(part, wbuf[:, pl.ds(base + PW, PW)], preferred_element_type=jnp.float32)
+        v = jnp.dot(part, wbuf[:, pl.ds(base + 2 * PW, PW)], preferred_element_type=jnp.float32)
+        for i in range(PW // HEAD):
+            kn[pl.ds(start, count), lanes_of(p, i)] = unit(k[:, i * HEAD : (i + 1) * HEAD])
+        vb[pl.ds(start, count), pl.ds(pl.multiple_of(p * PW, PW), PW)] = v.astype(jnp.bfloat16)
+
+    def attend(p):
+        for i in range(PW // HEAD):
+            lanes = lanes_of(p, i)
+            score = lax.dot_general(
+                qn[:, lanes],
+                kn[:, lanes],
+                (((1,), (1,)), ((), ())),
+                preferred_element_type=jnp.float32,
             )
-            v = jnp.dot(
-                nrm[...], wbuf[:, pl.ds(base + 2 * PW, PW)], preferred_element_type=jnp.float32
+            e = jnp.exp(score * scale) * mask
+            weight = (e / jnp.sum(e, axis=-1, keepdims=True)).astype(jnp.bfloat16)
+            att[:, lanes] = jnp.dot(
+                weight, vb[:, lanes], preferred_element_type=jnp.float32
             ).astype(jnp.bfloat16)
-            for i in range(PW // HEAD):
-                lanes = slice(i * HEAD, (i + 1) * HEAD)
-                score = lax.dot_general(
-                    unit(q[:, lanes]),
-                    unit(k[:, lanes]),
-                    (((1,), (1,)), ((), ())),
-                    preferred_element_type=jnp.float32,
-                ) * (HEAD ** (-0.5))
-                e = jnp.exp(score) * mask
-                weight = (e / jnp.sum(e, axis=-1, keepdims=True)).astype(jnp.bfloat16)
-                att[:, pl.ds(pl.multiple_of(p * PW + i * HEAD, HEAD), HEAD)] = jnp.dot(
-                    weight, v[:, lanes], preferred_element_type=jnp.float32
-                ).astype(jnp.bfloat16)
-            return carry
-
-        lax.fori_loop(0, PASSES, group, 0)
-
+
+    def finish(xr, outv, tick):
         def project(n, carry):
             lanes = pl.ds(pl.multiple_of(n * PW, PW), PW)
             outv[:, lanes] = (
@@ -292,15 +335,27 @@
         cp.start()
         return cp
 
+    def tick_one(p):
+        half = wbuf.at[pl.ds(0, 512), cols(p)]
+        pltpu.make_async_copy(half, half, sib_recv.at[p]).wait()
+        prepare(p, 0, ROWS, True)
+        attend(p)
+
+    load_gain.wait()
+    soon = [p for p in range(PASSES) if p not in HOLD]
+    for p in soon:
+        crossed(p)
     for b in range(LEVELS):
         e1[b].wait_recv()
     normalise(x1, 0, ROWS)
-    for p in range(PASSES):
-        half = wbuf.at[pl.ds(0, 512), cols(p)]
-        pltpu.make_async_copy(half, half, sib_recv.at[p]).wait()
+    for p in soon:
+        tick_one(p)
+    for p in HOLD:
+        crossed(p)
+        tick_one(p)
     load_wo.wait()
     load_arr.wait()
-    out1 = layer(x1, o1, 0)
+    out1 = finish(x1, o1, 0)
 
     rbuf[...] = jnp.where(sec == sections - 1, arr[...], o1[...])
     for b in range(1, LEVELS):
@@ -327,15 +382,29 @@
         0, send2.at[0], x2.at[pl.ds(RUN, BLOCK)], r_send.at[0], r_recv.at[0], sec, sib
     )
     e2[0].start()
-    for b in range(LEVELS):
+    EARLY = RUN + BLOCK
+    e2[0].wait_recv()
+    normalise(x2, 0, EARLY)
+
+    def early(p, carry):
+        prepare(p, 0, EARLY, True)
+        return carry
+
+    lax.fori_loop(0, PASSES, early, 0)
+    for b in range(1, LEVELS):
         e2[b].wait_recv()
-    normalise(x2, 0, ROWS)
-    out2 = layer(x2, o2, 1)
+    normalise(x2, EARLY, ROWS - EARLY)
+
+    def late(p, carry):
+        prepare(p, EARLY, ROWS - EARLY, False)
+        attend(p)
+        return carry
+
+    lax.fori_loop(0, PASSES, late, 0)
+    out2 = finish(x2, o2, 1)
 
     for p in range(PASSES):
-        zn = (2 * (NZ - 1)) if BOTH[p] else (NZ - 1)
-        xn = 1 if BOTH[p] else NZ
-        for n, sem in ((zn, z_send.at[p]), (xn, x_send.at[p]), (2 * NZ, sib_send.at[p])):
+        for n, sem in ((NZ - 1, z_send.at[p]), (NZ, x_send.at[p]), (2 * NZ, sib_send.at[p])):
             ref = wbuf.at[pl.ds(0, n * SHARD), cols(p)]
             pltpu.make_async_copy(ref, ref, sem).wait()
     for b in range(LEVELS):
@@ -350,20 +419,12 @@
     import functools
 
     anyspec = pl.BlockSpec(memory_space=pl.ANY)
-    vspec = pl.BlockSpec(memory_space=pltpu.VMEM)
     dma = pltpu.SemaphoreType.DMA
     bf = jnp.bfloat16
     return pl.pallas_call(
         functools.partial(kernel, sections),
         out_shape=jax.ShapeDtypeStruct((2, 1, RUN, D), bf),
-        in_specs=[
-            anyspec,
-            anyspec,
-            vspec,
-            anyspec,
-            anyspec,
-            pl.BlockSpec(memory_space=pltpu.SMEM),
-        ],
+        in_specs=[anyspec] * 6,
         out_specs=anyspec,
         scratch_shapes=[
             pltpu.VMEM((D, 3 * INNER), bf),
@@ -373,13 +434,18 @@
             pltpu.VMEM((RUN, D), bf),
             pltpu.VMEM((ROWS, D), bf),
             pltpu.VMEM((RUN, INNER), bf),
+            pltpu.VMEM((ROWS, INNER), bf),
+            pltpu.VMEM((ROWS, INNER), bf),
+            pltpu.VMEM((RUN, INNER), bf),
+            pltpu.VMEM((1, D), jnp.float32),
+            pltpu.VMEM(table.shape[::-1], jnp.int32),
             pltpu.VMEM((LEVELS, BLOCK, D), bf),
             pltpu.VMEM((LEVELS, BLOCK, D), bf),
             pltpu.VMEM((RUN, D), bf),
             pltpu.VMEM((RUN, D), bf),
             pltpu.VMEM((RUN, D), bf),
-            dma((15,)),
-            dma((4 * 9 * PASSES,)),
+            dma((17,)),
+            dma((2 * 9 * PASSES,)),
             dma((2 * 9 * PASSES,)),
             dma((PASSES,)),
             dma((PASSES,)),
@@ -394,7 +460,7 @@
         compiler_params=pltpu.CompilerParams(
             collective_id=0, has_side_effects=True, vmem_limit_bytes=56 * 1024 * 1024
         ),
-    )(x, arr, gain, w, wo, table)
+    )(x, arr, gain, w, wo, table.T)
 
 
 def solution(mesh):

time: 99.6 us -> 88.1 us (0.88); the launches traced: 99.3 us -> 86.5 us
  Pallas kernels: 96 us -> 84.6 us
  local copies, waits for them, and re-layouts: 3.25 us -> 1.87 us
    pallas_call x1, Pallas kernels: 96 us -> 84.6 us  [per_device(): pl.pallas_call(functools.partial(kernel, sections), out_shape=jax.ShapeDt...]
    unnamed x2 -> x1, local copies, waits for them, and re-layouts: 3.25 us -> 1.87 us
where the time goes in v2:
time: 88.1 us; the launch traced here: 86.5 us
  Pallas kernels  84.6 us (96%)
  local copies, waits for them, and re-layouts  1.87 us (2%)
    pallas_call x1, Pallas kernels, per_device(): pl.pallas_call(functools.partial(kernel, sections), out_shape=jax.ShapeDt...  84.6 us
    unnamed x1, local copies, waits for them, and re-layouts  1.87 us

profile of v2, /device:TPU:1, one launch (start us, length us, event | category | flops | bytes accessed | tf_op | source)
XLA Modules:
  0.0 86.5 jit_solution(13754358358420249590)
XLA Ops:
  0.0 84.6 %shard_map.64 = bf16[2,1,128,1024]{3,2,1,0:T(8,128)(2,1)} custom-call(bf16[1,128,1024]{2,1,0:T(8,128)(2,1)} %x_hbm.1, bf16[128,1024]{1,0:T(8,128)(2,1)} %arr_hbm.1, f32[1,1024]{1,0:T(1,128)} %gain_hbm.1, bf16[1,16,3072]{2,1,0:T(8,128)(2,1)} %w_hbm.1, bf16[1,1024,1024]{2,1,0:T(8,128)(2,1)} %wo_hbm.1, s32[4,64]{1,0:T(4,128)} %bitcast.1), custom_call_target="tpu_custom_call" | custom-call | tf_op jit(solution)/shard_map/pallas_call | solution.py:424
  84.6 1.9 %copy.8 = bf16[2,1,128,1024]{3,2,1,0:T(8,128)(2,1)} copy(bf16[2,1,128,1024]{3,2,1,0:T(8,128)(2,1)} %shard_map.64) | data formatting | bytes 1048576

commit v3 on v2

--- a/solution.py
+++ b/solution.py
@@ -19,8 +19,8 @@
 PW = 256
 ROWS = RUN + LEVELS * BLOCK
 EPS = 1e-06
-
-HOLD = ()
+NEAR = 2
+
 EXCHANGE_AT = (5, 5, 5)
 
 
@@ -91,7 +91,7 @@
     barrier = pltpu.get_barrier_semaphore()
     talk = [(sec, up), (sec, down), (sec, sib), (sec, across)]
     talk += [(sec, partners[b]) for b in range(1, LEVELS)]
-    talk += [(prv, me)] + [(prv, partners[b]) for b in range(1, LEVELS)]
+    talk += [(prv, me)] + [(prv, partners[b]) for b in range(NEAR, LEVELS)]
     for s, j in talk:
         pl.semaphore_signal(barrier, inc=1, device_id=dev(s, j))
 
@@ -137,6 +137,13 @@
         cp.wait()
     pl.semaphore_wait(barrier, len(talk))
 
+    def normalise(xr, start, count):
+        wide = xr[pl.ds(start, count), :].astype(jnp.float32)
+        ms = jnp.mean(wide * wide, axis=-1, keepdims=True)
+        nrm[pl.ds(start, count), :] = (wide * lax.rsqrt(ms + EPS) * gain_ref[...]).astype(
+            jnp.bfloat16
+        )
+
     def cols(p):
         return pl.ds(p * PCOLS, PCOLS)
 
@@ -182,79 +189,73 @@
         for b in range(LEVELS)
     ]
 
+    def ends(hh, s, p):
+        below = at(hh, (z + NZ - s) % NZ, c)
+        above = at(hh, (z + s) % NZ, c)
+        return (below, above) if p % 2 == 0 else (above, below)
+
+    def targets(p):
+        return (up, down) if p % 2 == 0 else (down, up)
+
     def begin():
         for p in range(PASSES):
-            push(me, p, z_send.at[p], zsem(0, 1, p), up)
-            push(me, p, z_send.at[p], zsem(1, 1, p), down)
+            long, short = targets(p)
+            push(me, p, z_send.at[p], zsem(0, 1, p), long)
+            push(me, p, z_send.at[p], zsem(1, 1, p), short)
         for p in range(PASSES):
-            if p not in HOLD:
-                push(me, p, x_send.at[p], xsem(0, 0, p), across)
+            push(me, p, x_send.at[p], xsem(0, 0, p), across)
         for p in range(PASSES):
             to_sib(me, p)
 
-    def held(p):
-        push(me, p, x_send.at[p], xsem(0, 0, p), across)
-
-        def one(s, carry):
-            below = at(h, (z + NZ - s) % NZ, c)
-            above = at(h, (z + s) % NZ, c)
-            push(below, p, x_send.at[p], xsem(0, s, p), across)
+    def ring(s):
+        for p in range(PASSES):
+            one, two = ends(h, s, p)
+            long, short = targets(p)
+            got(one, p, zsem(0, s, p))
 
             @pl.when(s < NZ // 2)
-            def _():
-                push(above, p, x_send.at[p], xsem(1, s, p), across)
-
-            return carry
-
-        lax.fori_loop(1, NZ // 2 + 1, one, 0)
-
-    def ring(s):
-        below = at(h, (z + NZ - s) % NZ, c)
-        above = at(h, (z + s) % NZ, c)
-        for p in range(PASSES):
-            got(below, p, zsem(0, s, p))
+            def _(p=p, one=one, long=long):
+                push(one, p, z_send.at[p], zsem(0, s + 1, p), long)
+
+            push(one, p, x_send.at[p], xsem(0, s, p), across)
+            to_sib(one, p)
 
             @pl.when(s < NZ // 2)
-            def _():
-                push(below, p, z_send.at[p], zsem(0, s + 1, p), up)
-
-            if p not in HOLD:
-                push(below, p, x_send.at[p], xsem(0, s, p), across)
-            to_sib(below, p)
-
-            @pl.when(s < NZ // 2)
-            def _(p=p):
-                got(above, p, zsem(1, s, p))
+            def _(p=p, two=two, short=short):
+                got(two, p, zsem(1, s, p))
 
                 @pl.when(s < NZ // 2 - 1)
                 def _():
-                    push(above, p, z_send.at[p], zsem(1, s + 1, p), down)
-
-                if p not in HOLD:
-                    push(above, p, x_send.at[p], xsem(1, s, p), across)
-                to_sib(above, p)
-
-    def crossed(p):
-        got(across, p, xsem(0, 0, p))
-        to_sib(across, p)
+                    push(two, p, z_send.at[p], zsem(1, s + 1, p), short)
+
+                push(two, p, x_send.at[p], xsem(1, s, p), across)
+                to_sib(two, p)
+
+    def crossed(lo, hi):
+        if lo == 0:
+            for p in range(PASSES):
+                got(across, p, xsem(0, 0, p))
+                to_sib(across, p)
 
         def one(s, carry):
-            below = at(1 - h, (z + NZ - s) % NZ, c)
-            above = at(1 - h, (z + s) % NZ, c)
-            got(below, p, xsem(0, s, p))
-            to_sib(below, p)
-
-            @pl.when(s < NZ // 2)
-            def _():
-                got(above, p, xsem(1, s, p))
-                to_sib(above, p)
+            for p in range(PASSES):
+                first, second = ends(1 - h, s, p)
+                got(first, p, xsem(0, s, p))
+                to_sib(first, p)
+
+                @pl.when(s < NZ // 2)
+                def _(p=p, second=second):
+                    got(second, p, xsem(1, s, p))
+                    to_sib(second, p)
 
             return carry
 
-        lax.fori_loop(1, NZ // 2 + 1, one, 0)
+        lax.fori_loop(max(lo, 1), hi, one, 0)
 
     begin()
     e1[0].start()
+    load_gain.wait()
+    normalise(x1, 0, RUN)
 
     def step(i, carry):
         ring(i)
@@ -267,8 +268,7 @@
         return carry
 
     lax.fori_loop(1, NZ // 2 + 1, step, 0)
-    for p in HOLD:
-        held(p)
+    crossed(0, 5)
 
     qrow = lax.broadcasted_iota(jnp.int32, (RUN, ROWS), 0)
     kcol = lax.broadcasted_iota(jnp.int32, (RUN, ROWS), 1)
@@ -278,13 +278,6 @@
     def unit(a):
         ms = jnp.mean(a * a, axis=-1, keepdims=True)
         return (a * lax.rsqrt(ms + EPS)).astype(jnp.bfloat16)
-
-    def normalise(xr, start, count):
-        wide = xr[pl.ds(start, count), :].astype(jnp.float32)
-        ms = jnp.mean(wide * wide, axis=-1, keepdims=True)
-        nrm[pl.ds(start, count), :] = (wide * lax.rsqrt(ms + EPS) * gain_ref[...]).astype(
-            jnp.bfloat16
-        )
 
     scale = HEAD ** (-0.5)
 
@@ -341,47 +334,39 @@
         prepare(p, 0, ROWS, True)
         attend(p)
 
-    load_gain.wait()
-    soon = [p for p in range(PASSES) if p not in HOLD]
-    for p in soon:
-        crossed(p)
     for b in range(LEVELS):
         e1[b].wait_recv()
-    normalise(x1, 0, ROWS)
-    for p in soon:
-        tick_one(p)
-    for p in HOLD:
-        crossed(p)
+    normalise(x1, RUN, ROWS - RUN)
+    crossed(5, NZ // 2 + 1)
+    for p in range(PASSES):
         tick_one(p)
     load_wo.wait()
     load_arr.wait()
     out1 = finish(x1, o1, 0)
 
     rbuf[...] = jnp.where(sec == sections - 1, arr[...], o1[...])
-    for b in range(1, LEVELS):
+    for b in range(NEAR, LEVELS):
         send2[b] = choose(rbuf, partners[b], b)
     relay = exch(0, rbuf, x2.at[pl.ds(0, RUN)], r_send.at[4], r_recv.at[4], nxt, me)
     relay.start()
-    e2 = [None] + [
+    e2 = [
         exch(
             b,
             send2.at[b],
             x2.at[pl.ds(RUN + b * BLOCK, BLOCK)],
             r_send.at[b],
             r_recv.at[b],
-            nxt,
+            sec if b < NEAR else nxt,
             partners[b],
         )
-        for b in range(1, LEVELS)
+        for b in range(LEVELS)
     ]
-    for b in (3, 2, 1):
+    for b in range(LEVELS - 1, NEAR - 1, -1):
         e2[b].start()
     relay.wait_recv()
-    send2[0] = choose(x2, sib, 0)
-    e2[0] = exch(
-        0, send2.at[0], x2.at[pl.ds(RUN, BLOCK)], r_send.at[0], r_recv.at[0], sec, sib
-    )
-    e2[0].start()
+    for b in range(NEAR - 1, -1, -1):
+        send2[b] = choose(x2, partners[b], b)
+        e2[b].start()
     EARLY = RUN + BLOCK
     e2[0].wait_recv()
     normalise(x2, 0, EARLY)

time: 88.1 us -> 87.4 us (level)
  no operation moved by 1% of the time
where the time goes in v3:
time: 87.4 us; the launch traced here: 86.4 us
  Pallas kernels  84.5 us (97%)
  local copies, waits for them, and re-layouts  1.87 us (2%)
    pallas_call x1, Pallas kernels, per_device(): pl.pallas_call(functools.partial(kernel, sections), out_shape=jax.ShapeDt...  84.5 us
    unnamed x1, local copies, waits for them, and re-layouts  1.87 us

profile of v3, /device:TPU:1, one launch (start us, length us, event | category | flops | bytes accessed | tf_op | source)
XLA Modules:
  0.0 86.4 jit_solution(13540903636258755668)
XLA Ops:
  0.0 84.5 %shard_map.64 = bf16[2,1,128,1024]{3,2,1,0:T(8,128)(2,1)} custom-call(bf16[1,128,1024]{2,1,0:T(8,128)(2,1)} %x_hbm.1, bf16[128,1024]{1,0:T(8,128)(2,1)} %arr_hbm.1, f32[1,1024]{1,0:T(1,128)} %gain_hbm.1, bf16[1,16,3072]{2,1,0:T(8,128)(2,1)} %w_hbm.1, bf16[1,1024,1024]{2,1,0:T(8,128)(2,1)} %wo_hbm.1, s32[4,64]{1,0:T(4,128)} %bitcast.1), custom_call_target="tpu_custom_call" | custom-call | tf_op jit(solution)/shard_map/pallas_call | solution.py:409
  84.5 1.9 %copy.8 = bf16[2,1,128,1024]{3,2,1,0:T(8,128)(2,1)} copy(bf16[2,1,128,1024]{3,2,1,0:T(8,128)(2,1)} %shard_map.64) | data formatting | bytes 1048576

commit v4 on v3

--- a/solution.py
+++ b/solution.py
@@ -20,6 +20,8 @@
 ROWS = RUN + LEVELS * BLOCK
 EPS = 1e-06
 NEAR = 2
+PARTS = 2
+PART = D // PARTS
 
 EXCHANGE_AT = (5, 5, 5)
 
@@ -37,7 +39,7 @@
     w_hbm,
     wo_hbm,
     table_hbm,
-    out_hbm,
+    out_ref,
     wbuf,
     wo,
     x1,
@@ -52,8 +54,6 @@
     table_ref,
     send1,
     send2,
-    o1,
-    o2,
     rbuf,
     load_sem,
     z_recv,
@@ -66,7 +66,6 @@
     e_recv,
     r_send,
     r_recv,
-    out_sem,
 ):
     sec = lax.axis_index("section")
     me = lax.axis_index("seq")
@@ -95,13 +94,13 @@
     for s, j in talk:
         pl.semaphore_signal(barrier, inc=1, device_id=dev(s, j))
 
-    def choose(ref, reader, level):
+    def choose(ref, reader, level, lanes):
         row = table_ref[pl.ds(level, 1), :].astype(jnp.float32)
         here = lax.broadcasted_iota(jnp.int32, row.shape, 1) == reader
         entry = jnp.sum(jnp.where(here, row, 0.0), axis=1, keepdims=True)
-        second = jnp.broadcast_to(entry, (BLOCK, D)) > 0.5
-        lower = ref[pl.ds(0, BLOCK), :].astype(jnp.float32)
-        upper = ref[pl.ds(BLOCK, BLOCK), :].astype(jnp.float32)
+        lower = ref[pl.ds(0, BLOCK), lanes].astype(jnp.float32)
+        upper = ref[pl.ds(BLOCK, BLOCK), lanes].astype(jnp.float32)
+        second = jnp.broadcast_to(entry, lower.shape) > 0.5
         return jnp.where(second, upper, lower).astype(jnp.bfloat16)
 
     def rows(slot):
@@ -132,7 +131,7 @@
     load_table.wait()
     load_x.wait()
     for b in range(LEVELS):
-        send1[b] = choose(x1, partners[b], b)
+        send1[b] = choose(x1, partners[b], b, slice(None))
     for cp in loads:
         cp.wait()
     pl.semaphore_wait(barrier, len(talk))
@@ -314,19 +313,16 @@
                 weight, vb[:, lanes], preferred_element_type=jnp.float32
             ).astype(jnp.bfloat16)
 
-    def finish(xr, outv, tick):
-        def project(n, carry):
-            lanes = pl.ds(pl.multiple_of(n * PW, PW), PW)
+    def project(xr, outv, part):
+        def one(n, carry):
+            lanes = pl.ds(pl.multiple_of(part * PART + n * PW, PW), PW)
             outv[:, lanes] = (
                 xr[pl.ds(0, RUN), lanes].astype(jnp.float32)
                 + jnp.dot(att[...], wo[:, lanes], preferred_element_type=jnp.float32)
             ).astype(jnp.bfloat16)
             return carry
 
-        lax.fori_loop(0, D // PW, project, 0)
-        cp = pltpu.make_async_copy(outv, out_hbm.at[tick, 0], out_sem.at[tick])
-        cp.start()
-        return cp
+        lax.fori_loop(0, PART // PW, one, 0)
 
     def tick_one(p):
         half = wbuf.at[pl.ds(0, 512), cols(p)]
@@ -342,33 +338,54 @@
         tick_one(p)
     load_wo.wait()
     load_arr.wait()
-    out1 = finish(x1, o1, 0)
-
-    rbuf[...] = jnp.where(sec == sections - 1, arr[...], o1[...])
-    for b in range(NEAR, LEVELS):
-        send2[b] = choose(rbuf, partners[b], b)
-    relay = exch(0, rbuf, x2.at[pl.ds(0, RUN)], r_send.at[4], r_recv.at[4], nxt, me)
-    relay.start()
-    e2 = [
-        exch(
-            b,
-            send2.at[b],
-            x2.at[pl.ds(RUN + b * BLOCK, BLOCK)],
-            r_send.at[b],
-            r_recv.at[b],
-            sec if b < NEAR else nxt,
-            partners[b],
+    o1 = out_ref.at[0, 0]
+    relay, e2 = [], []
+    for part in range(PARTS):
+        lanes = pl.ds(part * PART, PART)
+        sem = part * (LEVELS + 1)
+        relay.append(
+            exch(
+                0,
+                rbuf.at[:, lanes],
+                x2.at[pl.ds(0, RUN), lanes],
+                r_send.at[sem + LEVELS],
+                r_recv.at[sem + LEVELS],
+                nxt,
+                me,
+            )
         )
-        for b in range(LEVELS)
-    ]
-    for b in range(LEVELS - 1, NEAR - 1, -1):
-        e2[b].start()
-    relay.wait_recv()
-    for b in range(NEAR - 1, -1, -1):
-        send2[b] = choose(x2, partners[b], b)
-        e2[b].start()
+        e2.append(
+            [
+                exch(
+                    b,
+                    send2.at[b, :, lanes],
+                    x2.at[pl.ds(RUN + b * BLOCK, BLOCK), lanes],
+                    r_send.at[sem + b],
+                    r_recv.at[sem + b],
+                    sec if b < NEAR else nxt,
+                    partners[b],
+                )
+                for b in range(LEVELS)
+            ]
+        )
+    for part in range(PARTS):
+        lanes = pl.ds(part * PART, PART)
+        project(x1, o1, part)
+        rbuf[:, lanes] = jnp.where(sec == sections - 1, arr[:, lanes], o1[:, lanes])
+        for b in range(NEAR, LEVELS):
+            send2[b, :, lanes] = choose(rbuf, partners[b], b, lanes)
+        relay[part].start()
+        for b in range(LEVELS - 1, NEAR - 1, -1):
+            e2[part][b].start()
+    for part in range(PARTS):
+        lanes = pl.ds(part * PART, PART)
+        relay[part].wait_recv()
+        for b in range(NEAR - 1, -1, -1):
+            send2[b, :, lanes] = choose(x2, partners[b], b, lanes)
+            e2[part][b].start()
     EARLY = RUN + BLOCK
-    e2[0].wait_recv()
+    for part in range(PARTS):
+        e2[part][0].wait_recv()
     normalise(x2, 0, EARLY)
 
     def early(p, carry):
@@ -377,7 +394,8 @@
 
     lax.fori_loop(0, PASSES, early, 0)
     for b in range(1, LEVELS):
-        e2[b].wait_recv()
+        for part in range(PARTS):
+            e2[part][b].wait_recv()
     normalise(x2, EARLY, ROWS - EARLY)
 
     def late(p, carry):
@@ -386,7 +404,8 @@
         return carry
 
     lax.fori_loop(0, PASSES, late, 0)
-    out2 = finish(x2, o2, 1)
+    for part in range(PARTS):
+        project(x2, out_ref.at[1, 0], part)
 
     for p in range(PASSES):
         for n, sem in ((NZ - 1, z_send.at[p]), (NZ, x_send.at[p]), (2 * NZ, sib_send.at[p])):
@@ -394,10 +413,10 @@
             pltpu.make_async_copy(ref, ref, sem).wait()
     for b in range(LEVELS):
         e1[b].wait_send()
-        e2[b].wait_send()
-    relay.wait_send()
-    out1.wait()
-    out2.wait()
+        for part in range(PARTS):
+            e2[part][b].wait_send()
+    for part in range(PARTS):
+        relay[part].wait_send()
 
 
 def per_device(sections, x, arr, gain, w, wo, table):
@@ -410,7 +429,7 @@
         functools.partial(kernel, sections),
         out_shape=jax.ShapeDtypeStruct((2, 1, RUN, D), bf),
         in_specs=[anyspec] * 6,
-        out_specs=anyspec,
+        out_specs=pl.BlockSpec(memory_space=pltpu.VMEM),
         scratch_shapes=[
             pltpu.VMEM((D, 3 * INNER), bf),
             pltpu.VMEM((INNER, D), bf),
@@ -427,8 +446,6 @@
             pltpu.VMEM((LEVELS, BLOCK, D), bf),
             pltpu.VMEM((LEVELS, BLOCK, D), bf),
             pltpu.VMEM((RUN, D), bf),
-            pltpu.VMEM((RUN, D), bf),
-            pltpu.VMEM((RUN, D), bf),
             dma((17,)),
             dma((2 * 9 * PASSES,)),
             dma((2 * 9 * PASSES,)),
@@ -438,14 +455,13 @@
             dma((PASSES,)),
             dma((LEVELS,)),
             dma((LEVELS,)),
-            dma((LEVELS + 1,)),
-            dma((LEVELS + 1,)),
-            dma((2,)),
+            dma((PARTS * (LEVELS + 1),)),
+            dma((PARTS * (LEVELS + 1),)),
         ],
         compiler_params=pltpu.CompilerParams(
-            collective_id=0, has_side_effects=True, vmem_limit_bytes=56 * 1024 * 1024
+            collective_id=0, has_side_effects=True, vmem_limit_bytes=24 * 1024 * 1024
         ),
-    )(x, arr, gain, w, wo, table.T)
+    )(*[pltpu.with_memory_space_constraint(a, pltpu.HBM) for a in (x, arr, gain, w, wo, table.T)])
 
 
 def solution(mesh):

time: 87.4 us -> 84.6 us (0.968)
  local copies, waits for them, and re-layouts: 1.87 us -> 0.8 us
  Pallas kernels: 84.5 us -> 83.6 us
    unnamed x1, local copies, waits for them, and re-layouts: 1.87 us -> 0.8 us
    pallas_call x1, Pallas kernels: 84.5 us -> 83.6 us  [per_device(): pl.pallas_call(functools.partial(kernel, sections), out_shape=jax.ShapeDt...]
where the time goes in v4:
time: 84.6 us; the launch traced here: 84.4 us
  Pallas kernels  83.6 us (99%)
    pallas_call x1, Pallas kernels, per_device(): pl.pallas_call(functools.partial(kernel, sections), out_shape=jax.ShapeDt...  83.6 us

profile of v4, /device:TPU:1, one launch (start us, length us, event | category | flops | bytes accessed | tf_op | source)
XLA Modules:
  0.0 84.4 jit_solution(12678829455054721036)
XLA Ops:
  0.0 83.6 %shard_map.64 = bf16[2,1,128,1024]{3,2,1,0:T(8,128)(2,1)S(1)} custom-call(bf16[1,128,1024]{2,1,0:T(8,128)(2,1)} %x_hbm.1, bf16[128,1024]{1,0:T(8,128)(2,1)} %arr_hbm.1, f32[1,1024]{1,0:T(1,128)} %gain_hbm.1, bf16[1,16,3072]{2,1,0:T(8,128)(2,1)} %w_hbm.1, bf16[1,1024,1024]{2,1,0:T(8,128)(2,1)} %wo_hbm.1, s32[4,64]{1,0:T(4,128)} %bitcast.1), custom_call_target="tpu_custom_call" | custom-call | tf_op jit(solution)/shard_map/pallas_call | solution.py:428
  83.6 0.8 copy.8

commit v5 on v4

--- a/solution.py
+++ b/solution.py
@@ -269,10 +269,9 @@
     lax.fori_loop(1, NZ // 2 + 1, step, 0)
     crossed(0, 5)
 
-    qrow = lax.broadcasted_iota(jnp.int32, (RUN, ROWS), 0)
-    kcol = lax.broadcasted_iota(jnp.int32, (RUN, ROWS), 1)
-    seen = (kcol >= RUN) | ((kcol >= BLOCK) == (qrow >= BLOCK))
-    mask = jnp.where(seen, 1.0, 0.0).astype(jnp.float32)
+    qrow = lax.broadcasted_iota(jnp.int32, (RUN, RUN), 0)
+    kcol = lax.broadcasted_iota(jnp.int32, (RUN, RUN), 1)
+    mask = jnp.where((kcol >= BLOCK) == (qrow >= BLOCK), 1.0, 0.0).astype(jnp.float32)
 
     def unit(a):
         ms = jnp.mean(a * a, axis=-1, keepdims=True)
@@ -307,8 +306,10 @@
                 (((1,), (1,)), ((), ())),
                 preferred_element_type=jnp.float32,
             )
-            e = jnp.exp(score * scale) * mask
-            weight = (e / jnp.sum(e, axis=-1, keepdims=True)).astype(jnp.bfloat16)
+            e = jnp.exp(score * scale)
+            e = jnp.concatenate([e[:, :RUN] * mask, e[:, RUN:]], axis=1)
+            share = 1.0 / jnp.sum(e, axis=-1, keepdims=True)
+            weight = (e * share).astype(jnp.bfloat16)
             att[:, lanes] = jnp.dot(
                 weight, vb[:, lanes], preferred_element_type=jnp.float32
             ).astype(jnp.bfloat16)
@@ -396,7 +397,7 @@
     for b in range(1, LEVELS):
         for part in range(PARTS):
             e2[part][b].wait_recv()
-    normalise(x2, EARLY, ROWS - EARLY)
+        normalise(x2, RUN + b * BLOCK, BLOCK)
 
     def late(p, carry):
         prepare(p, EARLY, ROWS - EARLY, False)

time: 84.6 us -> 84.8 us (level)
  no operation moved by 1% of the time
where the time goes in v5:
time: 84.8 us; the launch traced here: 84.6 us
  Pallas kernels  83.8 us (99%)
    pallas_call x1, Pallas kernels, per_device(): pl.pallas_call(functools.partial(kernel, sections), out_shape=jax.ShapeDt...  83.8 us

profile of v5, /device:TPU:1, one launch (start us, length us, event | category | flops | bytes accessed | tf_op | source)
XLA Modules:
  0.0 84.6 jit_solution(3182526378619424325)
XLA Ops:
  0.0 83.8 %shard_map.64 = bf16[2,1,128,1024]{3,2,1,0:T(8,128)(2,1)S(1)} custom-call(bf16[1,128,1024]{2,1,0:T(8,128)(2,1)} %x_hbm.1, bf16[128,1024]{1,0:T(8,128)(2,1)} %arr_hbm.1, f32[1,1024]{1,0:T(1,128)} %gain_hbm.1, bf16[1,16,3072]{2,1,0:T(8,128)(2,1)} %w_hbm.1, bf16[1,1024,1024]{2,1,0:T(8,128)(2,1)} %wo_hbm.1, s32[4,64]{1,0:T(4,128)} %bitcast.1), custom_call_target="tpu_custom_call" | custom-call | tf_op jit(solution)/shard_map/pallas_call | solution.py:429
  83.8 0.8 copy.8

commit v6 on v4

--- a/solution.py
+++ b/solution.py
@@ -23,7 +23,7 @@
 PARTS = 2
 PART = D // PARTS
 
-EXCHANGE_AT = (5, 5, 5)
+EXCHANGE_AT = (6, 6, 6)
 
 
 def flip(i, bit):

time: 84.6 us -> 84.1 us (level)
  no operation moved by 1% of the time
where the time goes in v6:
time: 84.1 us; the launch traced here: 84 us
  Pallas kernels  83.2 us (99%)
    pallas_call x1, Pallas kernels, per_device(): pl.pallas_call(functools.partial(kernel, sections), out_shape=jax.ShapeDt...  83.2 us

profile of v6, /device:TPU:1, one launch (start us, length us, event | category | flops | bytes accessed | tf_op | source)
XLA Modules:
  0.0 84.0 jit_solution(7505340158893740613)
XLA Ops:
  0.0 83.2 %shard_map.64 = bf16[2,1,128,1024]{3,2,1,0:T(8,128)(2,1)S(1)} custom-call(bf16[1,128,1024]{2,1,0:T(8,128)(2,1)} %x_hbm.1, bf16[128,1024]{1,0:T(8,128)(2,1)} %arr_hbm.1, f32[1,1024]{1,0:T(1,128)} %gain_hbm.1, bf16[1,16,3072]{2,1,0:T(8,128)(2,1)} %w_hbm.1, bf16[1,1024,1024]{2,1,0:T(8,128)(2,1)} %wo_hbm.1, s32[4,64]{1,0:T(4,128)} %bitcast.1), custom_call_target="tpu_custom_call" | custom-call | tf_op jit(solution)/shard_map/pallas_call | solution.py:428
  83.2 0.8 copy.8
